TPU v7x, 32 devices: a whole 2x2x4 slice. The times are simulated.
32 devices in a mesh: loop: 4 (over y, x), bulk: 8 (over z, core).
Axes of the slice: x: 2, y: 2, z: 4, core: 2. Of those that a mesh axis runs over, the one named last changes fastest.
Arguments:
- series: float32 [4224, 3072], P('loop', 'bulk'), may hold values from -64 to 64
Outputs:
- correlation: float32 [4, 1056, 4224], P(None, 'bulk', 'loop')
All inputs are finite; a program needn't handle non-finite values.
Results may differ from a plain program's by a relative error of at most 0.0011.
Values may be sent and summed in bfloat16 or wider, within the bound.
A program may use at most 64 MiB of HBM per device.

v0:
```python
import jax
import jax.numpy as jnp
from jax import lax
from jax.sharding import PartitionSpec as P

TIME = 3072
epsilon = 1e-06


def normalize(centered, square_total):
    return (centered * lax.rsqrt(square_total / TIME + epsilon)).astype(jnp.bfloat16)


def contract(first_operand, second_operand):
    product = lax.dot_general(
        first_operand, second_operand, (((1,), (1,)), ((), ())), preferred_element_type=jnp.float32
    )
    return product / TIME


def cycle_gather(own_rows):
    return lax.all_gather(own_rows, "loop", axis=0, tiled=True)


def on_device(series):
    share_rows = series.shape[0] // lax.axis_size("bulk")
    average = lax.psum(jnp.sum(series, axis=1, keepdims=True), "bulk") / TIME
    centered = series - average
    squares = lax.psum(jnp.sum(centered * centered, axis=1, keepdims=True), "bulk")
    zscore = normalize(centered, squares)
    row_series = lax.all_gather(zscore, "bulk", axis=1, tiled=True)
    own_rows = lax.dynamic_slice_in_dim(
        row_series, lax.axis_index("bulk") * share_rows, share_rows, 0
    )
    gathered = contract(cycle_gather(own_rows), row_series)
    return gathered.reshape(lax.axis_size("loop"), share_rows, series.shape[0])


def solution(mesh):
    placed = (P("loop", "bulk"),)
    return jax.shard_map(
        on_device, mesh=mesh, in_specs=placed, out_specs=P(None, "bulk", "loop"), check_vma=False
    )
```

profile of v0, /device:TPU:0, one launch (start us, length us, event | category | flops | bytes accessed | tf_op | source)
XLA Modules:
  0.0 174.9 jit_solution(680406850263193112)
XLA Ops:
  6.5 0.0 copy-start
  6.5 0.0 all-gather.4.cloned.1.call-start
  6.5 1.8 %reduce_sum.18 = f32[1056]{0:T(1024)S(1)} reduce(f32[1056,384]{1,0:T(8,128)} %param.1, f32[]{:T(128)} %constant.7.clone.1), dimensions={1}, to_apply=%region_0.0 | reduce | flops 404448 | bytes 1626244 | tf_op jit(solution)/shard_map/reduce_sum | solution.py:27
  8.3 18.3 %psum.14 = f32[1056,1]{0,1:T(1,128)S(1)} all-reduce(f32[1056,1]{0,1:T(1,128)S(1)} %broadcast_in_dim.6), channel_id=1, replica_groups=mesh['loop'=4,'bulk'=8] {'bulk'}, use_global_device_ids=true, to_apply=%region_1.0 | all-reduce | flops 1056 | bytes 8448 | tf_op jit(solution)/shard_map/psum | solution.py:27
  26.7 0.0 copy-done
  26.7 0.4 multiply_reduce_fusion
  27.1 13.9 %psum.15 = f32[1056,1]{0,1:T(1,128)S(1)} all-reduce(f32[1056,1]{0,1:T(1,128)S(1)} %broadcast_in_dim.7), channel_id=1, replica_groups=mesh['loop'=4,'bulk'=8] {'bulk'}, use_global_device_ids=true, to_apply=%region_3.0 | all-reduce | flops 1056 | bytes 8448 | tf_op jit(solution)/shard_map/psum | solution.py:29
  41.1 1.2 multiply_convert_fusion
  42.3 0.0 all-gather.4.cloned.1.call-update
  42.3 0.0 all-gather.6.cloned.1.call-start
  42.4 64.4 %all-gather.4.cloned.1.call-done = bf16[1056,3072]{1,0:T(8,128)(2,1)} async-done(((bf16[1056,384]{1,0:T(8,128)(2,1)}), bf16[1056,3072]{1,0:T(8,128)(2,1)}) %all-gather.4.cloned.1.call-update) | async-done | bytes 6488080 | tf_op jit(solution)/shard_map/all_gather | solution.py:31
  106.8 2.3 %dynamic-slice_bitcast_fusion = bf16[1,132,3072]{2,1,0:T(8,128)(2,1)} fusion(bf16[1056,3072]{1,0:T(8,128)(2,1)} %all-gather.4.cloned.1.call-done, s32[]{:T(128)S(6)} %select_n.3), kind=kLoop, calls=%fused_computation.3 | loop fusion | bytes 1622020
  109.0 0.0 all-gather.6.cloned.1.call-update
  109.1 44.2 %all-gather.6.cloned.1.call-done = bf16[4,132,3072]{2,1,0:T(8,128)(2,1)} async-done(((bf16[1,132,3072]{2,1,0:T(8,128)(2,1)}), bf16[4,132,3072]{2,1,0:T(8,128)(2,1)}) %all-gather.6.cloned.1.call-update) | async-done | bytes 3244048 | tf_op jit(solution)/shard_map/all_gather | solution.py:22
  153.3 2.3 %reshape.5 = bf16[528,3072]{1,0:T(8,128)(2,1)S(1)} reshape(bf16[4,132,3072]{2,1,0:T(8,128)(2,1)} %all-gather.6.cloned.1.call-done) | data formatting | bytes 6488064
  155.6 8.7 %convolution_multiply_fusion = f32[528,1056]{1,0:T(8,128)} fusion(bf16[528,3072]{1,0:T(8,128)(2,1)S(1)} %reshape.5, bf16[1056,3072]{1,0:T(8,128)(2,1)} %all-gather.4.cloned.1.call-done), kind=kOutput, calls=%fused_computation | convolution fusion | flops 3426255360 | bytes 11962368 | tf_op jit(solution)/shard_map/dot_general | solution.py:15
  164.2 1.8 %reshape.3 = f32[4,132,1056]{2,1,0:T(8,128)S(1)} reshape(f32[528,1056]{1,0:T(8,128)} %convolution_multiply_fusion) | data formatting | bytes 4460544 | tf_op jit(solution)/shard_map/reshape | solution.py:36
  166.0 2.1 %copy.4 = f32[4,132,1056]{2,0,1:T(4,128)} copy(f32[4,132,1056]{2,1,0:T(8,128)S(1)} %reshape.3) | data formatting | bytes 4460544 | tf_op jit(solution)/shard_map/reshape | solution.py:36
  (4 shorter events, 0.1 us)
Async XLA Ops:
  6.5 20.2 %copy-start = (f32[1056,384]{1,0:T(8,128)S(1)}, f32[1056,384]{1,0:T(8,128)}, u32[]{:S(2)}) copy-start(f32[1056,384]{1,0:T(8,128)} %param.1) | copy-start | bytes 4866052
  6.5 100.2 %all-gather.4.cloned.1.call-start = ((), (), s32[]{:S(2)}) async-start(), calls=%async_computation | async-start | bytes 7299072 | tf_op jit(solution)/shard_map/all_gather | solution.py:31
  42.3 110.9 %all-gather.6.cloned.1.call-start = ((), (), s32[]{:S(2)}) async-start(), calls=%async_computation.1 | async-start | bytes 4177920 | tf_op jit(solution)/shard_map/all_gather | solution.py:22
Sparse Core Ops, SparseCore 0:
  42.5 64.2 all-gather.3
  109.2 44.0 all-gather.5
where the time goes:
time: 175 us
  waiting for transfers between devices  109 us (62%)
  blocking collectives  32.3 us (18%)
  between operations  13.5 us (8%)
  matrix products  8.65 us (5%)
  local copies, waits for them, and re-layouts  8.41 us (5%)
  other arithmetic  3.46 us (2%)
    all_gather x1, waiting for transfers between devices, on_device(): row_series = lax.all_gather(zscore, 'bulk', axis=1, tiled=True)  64.4 us
    all_gather x1, waiting for transfers between devices, cycle_gather(): return lax.all_gather(own_rows, 'loop', axis=0, tiled=True)  44.2 us
    psum x1, blocking collectives, on_device(): average = lax.psum(jnp.sum(series, axis=1, keepdims=True), 'bulk') / TIME  18.3 us
    psum x1, blocking collectives, on_device(): lax.psum(jnp.sum(centered * centered, axis=1, keepdims=True), 'bulk')  13.9 us
    dot_general x1, matrix products, contract(): lax.dot_general(first_operand, second_operand, (((1,), (1,)), ((), ())),...  8.65 us
    unnamed x4, local copies, waits for them, and re-layouts  4.55 us
    reshape x2, local copies, waits for them, and re-layouts, on_device(): return gathered.reshape(lax.axis_size('loop'), share_rows, series.shape[0])  3.84 us
  transfers between devices with their start and end apart: 2, of which 2 were waited for; matrix products, arithmetic and copies ran while one was open for 0% of the time, Pallas kernels for 0%

commit v1 on v0

--- a/solution.py
+++ b/solution.py
@@ -26,7 +26,9 @@
     share_rows = series.shape[0] // lax.axis_size("bulk")
     average = lax.psum(jnp.sum(series, axis=1, keepdims=True), "bulk") / TIME
     centered = series - average
-    squares = lax.psum(jnp.sum(centered * centered, axis=1, keepdims=True), "bulk")
+    squares = jnp.sum(
+        lax.all_gather(jnp.sum(centered * centered, axis=1, keepdims=True), "bulk"), axis=0
+    )
     zscore = normalize(centered, squares)
     row_series = lax.all_gather(zscore, "bulk", axis=1, tiled=True)
     own_rows = lax.dynamic_slice_in_dim(

time: 175 us -> 189 us (1.080)
  blocking collectives: 32.3 us -> 44.6 us
    unnamed x0 -> x1, blocking collectives: none -> 26.3 us
    psum x1 -> x0, blocking collectives: 13.9 us -> none  [on_device(): lax.psum(jnp.sum(centered * centered, axis=1, keepdims=True), 'bulk')]
    unnamed x4 -> x9, local copies, waits for them, and re-layouts: 4.55 us -> 5.47 us
where the time goes in v1:
time: 189 us
  waiting for transfers between devices  109 us (58%)
  blocking collectives  44.6 us (24%)
  between operations  14.1 us (7%)
  local copies, waits for them, and re-layouts  9.41 us (5%)
  matrix products  8.66 us (5%)
  other arithmetic  3.47 us (2%)
    all_gather x1, waiting for transfers between devices, on_device(): row_series = lax.all_gather(zscore, 'bulk', axis=1, tiled=True)  64.4 us
    all_gather x1, waiting for transfers between devices, cycle_gather(): return lax.all_gather(own_rows, 'loop', axis=0, tiled=True)  44.2 us
    unnamed x1, blocking collectives  26.3 us
    psum x1, blocking collectives, on_device(): average = lax.psum(jnp.sum(series, axis=1, keepdims=True), 'bulk') / TIME  18.3 us
    dot_general x1, matrix products, contract(): lax.dot_general(first_operand, second_operand, (((1,), (1,)), ((), ())),...  8.66 us
    unnamed x9, local copies, waits for them, and re-layouts  5.47 us
    reshape x2, local copies, waits for them, and re-layouts, on_device(): return gathered.reshape(lax.axis_size('loop'), share_rows, series.shape[0])  3.84 us
  transfers between devices with their start and end apart: 2, of which 2 were waited for; matrix products, arithmetic and copies ran while one was open for 0% of the time, Pallas kernels for 0%

profile of v1, /device:TPU:0, one launch (start us, length us, event | category | flops | bytes accessed | tf_op | source)
XLA Modules:
  0.0 189.0 jit_solution(8914373802729485387)
XLA Ops:
  6.5 0.0 copy-start.1
  6.5 0.0 copy-start
  6.5 0.0 all-gather.5.cloned.1.call-start
  6.5 1.8 reduce_sum.27
  8.3 18.3 %psum.7 = f32[1056,1]{0,1:T(1,128)S(1)} all-reduce(f32[1056,1]{0,1:T(1,128)S(1)} %broadcast_in_dim.3), channel_id=1, replica_groups=mesh['loop'=4,'bulk'=8] {'bulk'}, use_global_device_ids=true, to_apply=%region_1.0 | all-reduce | flops 1056 | bytes 8448 | tf_op jit(solution)/shard_map/psum | solution.py:27
  26.7 0.0 copy-done
  26.7 0.4 multiply_reduce_fusion
  27.1 0.0 copy-done.1
  27.1 0.6 dynamic-slice
  28.4 0.3 dynamic-update-slice
  28.7 26.3 %all-reduce = f32[8448]{0:T(1024)S(1)} all-reduce(f32[8448]{0:T(1024)S(1)} %dynamic-update-slice), channel_id=2, replica_groups=mesh['loop'=4,'bulk'=8] {'bulk'}, use_global_device_ids=true, to_apply=%add | all-reduce | flops 8448 | bytes 67584
  55.0 0.1 reshape.13
  55.1 1.2 multiply_convert_fusion
  56.4 0.0 all-gather.5.cloned.1.call-update
  56.4 0.0 all-gather.7.cloned.1.call-start
  56.4 64.4 %all-gather.5.cloned.1.call-done = bf16[1056,3072]{1,0:T(8,128)(2,1)} async-done(((bf16[1056,384]{1,0:T(8,128)(2,1)}), bf16[1056,3072]{1,0:T(8,128)(2,1)}) %all-gather.5.cloned.1.call-update) | async-done | bytes 6488080 | tf_op jit(solution)/shard_map/all_gather | solution.py:33
  120.8 2.3 %dynamic-slice_bitcast_fusion = bf16[1,132,3072]{2,1,0:T(8,128)(2,1)} fusion(bf16[1056,3072]{1,0:T(8,128)(2,1)} %all-gather.5.cloned.1.call-done, s32[]{:T(128)S(6)} %select_n.3), kind=kLoop, calls=%fused_computation.3 | loop fusion | bytes 1622020
  123.1 0.0 all-gather.7.cloned.1.call-update
  123.1 44.2 %all-gather.7.cloned.1.call-done = bf16[4,132,3072]{2,1,0:T(8,128)(2,1)} async-done(((bf16[1,132,3072]{2,1,0:T(8,128)(2,1)}), bf16[4,132,3072]{2,1,0:T(8,128)(2,1)}) %all-gather.7.cloned.1.call-update) | async-done | bytes 3244048 | tf_op jit(solution)/shard_map/all_gather | solution.py:22
  167.3 2.3 %reshape.19 = bf16[528,3072]{1,0:T(8,128)(2,1)S(1)} reshape(bf16[4,132,3072]{2,1,0:T(8,128)(2,1)} %all-gather.7.cloned.1.call-done) | data formatting | bytes 6488064
  169.6 8.7 %convolution_multiply_fusion = f32[528,1056]{1,0:T(8,128)} fusion(bf16[528,3072]{1,0:T(8,128)(2,1)S(1)} %reshape.19, bf16[1056,3072]{1,0:T(8,128)(2,1)} %all-gather.5.cloned.1.call-done), kind=kOutput, calls=%fused_computation | convolution fusion | flops 3426255360 | bytes 11962368 | tf_op jit(solution)/shard_map/dot_general | solution.py:15
  178.3 1.8 reshape.12
  180.1 2.1 %copy.5 = f32[4,132,1056]{2,0,1:T(4,128)} copy(f32[4,132,1056]{2,1,0:T(8,128)S(1)} %reshape.12) | data formatting | bytes 4460544 | tf_op jit(solution)/shard_map/reshape | solution.py:38
  (5 shorter events, 0.1 us)
Async XLA Ops:
  6.5 20.6 %copy-start.1 = (u32[32]{0:T(128)S(1)}, u32[32]{0:T(128)}, u32[]{:S(2)}) copy-start(u32[32]{0:T(128)} %constant.22) | copy-start | bytes 388
  6.5 20.2 %copy-start = (f32[1056,384]{1,0:T(8,128)S(1)}, f32[1056,384]{1,0:T(8,128)}, u32[]{:S(2)}) copy-start(f32[1056,384]{1,0:T(8,128)} %param.1) | copy-start | bytes 4866052
  6.5 114.3 %all-gather.5.cloned.1.call-start = ((), (), s32[]{:S(2)}) async-start(), calls=%async_computation | async-start | bytes 7299072 | tf_op jit(solution)/shard_map/all_gather | solution.py:33
  56.4 110.9 %all-gather.7.cloned.1.call-start = ((), (), s32[]{:S(2)}) async-start(), calls=%async_computation.1 | async-start | bytes 4177920 | tf_op jit(solution)/shard_map/all_gather | solution.py:22
Sparse Core Ops, SparseCore 0:
  56.5 64.2 all-gather.4
  123.2 44.0 all-gather.6
